TPU v7x, 512 devices: a whole 4x4x16 slice. The times are simulated.
512 devices in a mesh: leaf: 128 (over y, z, core), panel: 4 (over x).
Axes of the slice: x: 4, y: 4, z: 16, core: 2. Of those that a mesh axis runs over, the one named last changes fastest.
Arguments:
- border: bfloat16 [128, 128, 8192], P('leaf', 'panel'), may hold values from -0.046875 to 0.046875
- solution: bfloat16 [128, 128, 128], P('leaf', 'panel'), may hold values from -6 to 6
- winv_top: bfloat16 [4096, 4096], P(None, ('leaf', 'panel')), as said below
- winv_mid: bfloat16 [4096, 8192], P(None, ('leaf', 'panel')), as said below
- coupling: bfloat16 [8192, 4096], P(('leaf', 'panel')), may hold values from -0.0625 to 0.0625
Outputs:
- top_adjoint: float32 [4096, 128], P(('leaf', 'panel'))
- mid_adjoint: float32 [8192, 128], P(('leaf', 'panel'))
Inputs may be any that keep to these rules, and one draw needn't show every extreme that they name: `winv_top`: each 4096 x 4096 block of the factor is lower triangular with a positive diagonal. `winv_mid`: each 4096 x 4096 block of the factor is lower triangular with a positive diagonal.
All inputs are finite; a program needn't handle non-finite values.
Results may differ from a plain program's by a relative error of at most 0.0003.
Values sent between devices are 32-bit elements; how exact they have to be, the bound alone decides.
A program may use at most 64 MiB of HBM per device.

v0:
```python
import jax
import jax.numpy as jnp
from jax import lax
from jax.sharding import PartitionSpec as P


def from_partner(value, axis, stride):
    mask = 2**stride
    pairs = [(source, source ^ mask) for source in range(lax.axis_size(axis))]
    return lax.ppermute(value, axis, pairs)


def split_half(buffer, chosen):
    half_rows = buffer.shape[0] // 2
    kept_half = lax.dynamic_slice_in_dim(buffer, chosen * half_rows, half_rows, 0)
    sent_half = lax.dynamic_slice_in_dim(buffer, (1 - chosen) * half_rows, half_rows, 0)
    return (kept_half, sent_half)


def split_parity(buffer, chosen):
    paired = buffer.reshape(buffer.shape[0] // 2, 2, buffer.shape[1])
    even_rows = paired[:, 0]
    odd_rows = paired[:, 1]
    kept_rows = jnp.where(chosen == 0, even_rows, odd_rows)
    sent_rows = jnp.where(chosen == 0, odd_rows, even_rows)
    return (kept_rows, sent_rows)


def partner_halving(top_part, mid_part, leaf_id, leaf_bits):
    for bit_pos in reversed(range(leaf_bits)):
        chosen = leaf_id >> bit_pos & 1
        outgoing = []
        top_part, sent_top = split_half(top_part, chosen)
        outgoing.append(sent_top)
        if bit_pos < leaf_bits - 1:
            mid_part, sent_mid = split_half(mid_part, chosen)
            outgoing.append(sent_mid)
        received = from_partner(jnp.concatenate(outgoing, 0), "leaf", bit_pos)
        position = 0
        top_part = top_part + received[: top_part.shape[0]]
        position = top_part.shape[0]
        if bit_pos < leaf_bits - 1:
            mid_part = mid_part + received[position:]
    return (top_part, mid_part)


def body(border, solution, winv_top, winv_mid, coupling):
    leaves = lax.axis_size("leaf")
    leaf_bits = leaves.bit_length() - 1
    front_rows = winv_top.shape[0]
    leaf_id = lax.axis_index("leaf")
    contribution = lax.dot_general(
        border[0], solution[0], (((0,), (0,)), ((), ())), preferred_element_type=jnp.float32
    )
    top_part = contribution[:front_rows]
    mid_part = contribution[front_rows:]
    top_block, mid_block = partner_halving(top_part, mid_part, leaf_id, leaf_bits)
    top_block, mid_block = (
        lax.psum_scatter(top_block, "panel", scatter_dimension=0, tiled=True),
        lax.psum_scatter(mid_block, "panel", scatter_dimension=0, tiled=True),
    )
    top_factor = winv_top.astype(jnp.float32)
    top_inner = lax.psum(
        jnp.dot(top_factor, top_block, precision=lax.Precision.HIGHEST), ("leaf", "panel")
    )
    top_adjoint = jnp.dot(top_factor.T, top_inner, precision=lax.Precision.HIGHEST)
    top_whole = lax.all_gather(top_adjoint, ("leaf", "panel"), axis=0, tiled=True)
    couple = coupling.astype(jnp.float32)
    mid_rhs = mid_block - jnp.dot(couple, top_whole, precision=lax.Precision.HIGHEST)
    mid_factor = winv_mid.astype(jnp.float32)
    group_block = jnp.dot(mid_factor, mid_rhs, precision=lax.Precision.HIGHEST)
    for bit_pos in reversed(range(leaf_bits - 1)):
        chosen = leaf_id >> bit_pos & 1
        kept_rows, sent_rows = split_parity(group_block, chosen)
        group_block = kept_rows + from_partner(sent_rows, "leaf", bit_pos)
    group_block = lax.psum(group_block, "panel")
    for bit_pos in range(leaf_bits - 1):
        chosen = leaf_id >> bit_pos & 1
        received = from_partner(group_block, "leaf", bit_pos)
        even_rows = jnp.where(chosen == 0, group_block, received)
        odd_rows = jnp.where(chosen == 0, received, group_block)
        group_block = jnp.stack([even_rows, odd_rows], 1).reshape(
            2 * group_block.shape[0], group_block.shape[1]
        )
    mid_adjoint = jnp.dot(mid_factor.T, group_block, precision=lax.Precision.HIGHEST)
    return (top_adjoint, mid_adjoint)


def solution(mesh):
    placed = (
        P("leaf", "panel", None),
        P("leaf", "panel", None),
        P(None, ("leaf", "panel")),
        P(None, ("leaf", "panel")),
        P(("leaf", "panel"), None),
    )
    return jax.shard_map(
        body,
        mesh=mesh,
        in_specs=placed,
        out_specs=(P(("leaf", "panel"), None), P(("leaf", "panel"), None)),
        check_vma=False,
    )
```

profile of v0, /device:TPU:1, one launch (start us, length us, event | category | flops | bytes accessed | tf_op | source)
XLA Modules:
  0.0 1222.7 jit_solution(14282266658055465502)
XLA Ops:
  10.5 1.6 fusion.6
  12.1 2.3 constant_dynamic-slice_fusion.12
  14.4 5.6 collective-permute-start
  20.1 19.9 %collective-permute-done = f32[2048,128]{1,0:T(8,128)} collective-permute-done((f32[2048,128]{1,0:T(8,128)}, f32[2048,128]{1,0:T(8,128)}, u32[]{:S(2)}, u32[]{:S(2)}) %collective-permute-start) | collective-permute-done | bytes 1048608 | tf_op jit(solution)/shard_map/ppermute | solution.py:10
  42.9 6.2 collective-permute-start.1
  49.1 33.1 %collective-permute-done.1 = f32[3072,128]{1,0:T(8,128)} collective-permute-done((f32[3072,128]{1,0:T(8,128)}, f32[3072,128]{1,0:T(8,128)}, u32[]{:S(2)}, u32[]{:S(2)}) %collective-permute-start.1) | collective-permute-done | bytes 1572896 | tf_op jit(solution)/shard_map/ppermute | solution.py:10
  85.1 15.7 %collective-permute-start.2 = (f32[1536,128]{1,0:T(8,128)S(1)}, f32[1536,128]{1,0:T(8,128)S(1)}, u32[]{:S(2)}, u32[]{:S(2)}) collective-permute-start(f32[1536,128]{1,0:T(8,128)S(1)} %pad_maximum_fusion.3), channel_id=1, source_target_pairs={{0,64},{4,68},{8,72},{12,76},{16,80},{20,84},{24,88},{28,92},{32,9... | collective-permute-start | bytes 2359304 | tf_op jit(solution)/shard_map/ppermute | solution.py:10
  100.8 24.3 %collective-permute-done.2 = f32[1536,128]{1,0:T(8,128)S(1)} collective-permute-done((f32[1536,128]{1,0:T(8,128)S(1)}, f32[1536,128]{1,0:T(8,128)S(1)}, u32[]{:S(2)}, u32[]{:S(2)}) %collective-permute-start.2) | collective-permute-done | bytes 786464 | tf_op jit(solution)/shard_map/ppermute | solution.py:10
  126.4 38.8 %collective-permute-start.3 = (f32[768,128]{1,0:T(8,128)S(1)}, f32[768,128]{1,0:T(8,128)S(1)}, u32[]{:S(2)}, u32[]{:S(2)}) collective-permute-start(f32[768,128]{1,0:T(8,128)S(1)} %pad_maximum_fusion.5), channel_id=1, source_target_pairs={{0,32},{4,36},{8,40},{12,44},{16,48},{20,52},{24,56},{28,60},{32,0... | collective-permute-start | bytes 1179656 | tf_op jit(solution)/shard_map/ppermute | solution.py:10
  165.2 38.6 %collective-permute-done.3 = f32[768,128]{1,0:T(8,128)S(1)} collective-permute-done((f32[768,128]{1,0:T(8,128)S(1)}, f32[768,128]{1,0:T(8,128)S(1)}, u32[]{:S(2)}, u32[]{:S(2)}) %collective-permute-start.3) | collective-permute-done | bytes 393248 | tf_op jit(solution)/shard_map/ppermute | solution.py:10
  203.9 1.9 collective-permute-start.4
  205.9 9.6 collective-permute-done.4
  215.6 1.9 collective-permute-start.5
  217.6 3.8 collective-permute-done.5
  221.5 3.3 collective-permute-start.6
  226.7 13.1 %all-reduce = f32[32,128]{1,0:T(8,128)S(1)} all-reduce(f32[32,128]{1,0:T(8,128)S(1)} %slice_add_fusion.11), channel_id=2, replica_groups=mesh['leaf'=128,'panel'=4] {'panel'}, use_global_device_ids=true, to_apply=%region_0.0.clone | all-reduce | flops 4096 | bytes 32768
  239.8 2.4 convolution_bitcast_fusion.1
  242.3 481.7 %all-reduce.3.cloned.1.call-done = f32[4096,128]{0,1:T(8,128)} async-done(((f32[4096,128]{0,1:T(8,128)}), f32[4096,128]{0,1:T(8,128)}) %all-reduce.3.cloned.1.call-update) | async-done | bytes 2097168 | tf_op jit(solution)/shard_map/psum | solution.py:63
  724.0 3.2 convolution_bitcast_fusion.4
  727.9 194.9 %all-gather.2.cloned.1.call-done = f32[4096,128]{1,0:T(8,128)} async-done(((f32[8,128]{1,0:T(8,128)}), f32[4096,128]{1,0:T(8,128)}) %all-gather.2.cloned.1.call-update) | async-done | bytes 2097168 | tf_op jit(solution)/shard_map/all_gather | solution.py:67
  922.8 2.4 convolution_bitcast_fusion.3
  925.2 3.1 convolution_bitcast_fusion
  928.3 1.9 copy.66
  930.2 2.5 broadcast_select_fusion
  932.8 3.2 collective-permute-start.7
  936.0 23.3 %collective-permute-done.7 = f32[2048,128]{1,0:T(8,128)S(1)} collective-permute-done((f32[2048,128]{1,0:T(8,128)}, f32[2048,128]{1,0:T(8,128)S(1)}, u32[]{:S(2)}, u32[]{:S(2)}) %collective-permute-start.7) | collective-permute-done | bytes 1048608 | tf_op jit(solution)/shard_map/ppermute | solution.py:10
  961.4 7.0 collective-permute-start.8
  968.4 39.4 %collective-permute-done.8 = f32[1024,128]{1,0:T(8,128)S(1)} collective-permute-done((f32[1024,128]{1,0:T(8,128)S(1)}, f32[1024,128]{1,0:T(8,128)S(1)}, u32[]{:S(2)}, u32[]{:S(2)}) %collective-permute-start.8) | collective-permute-done | bytes 524320 | tf_op jit(solution)/shard_map/ppermute | solution.py:10
  1008.3 1.9 collective-permute-start.9
  1010.2 16.4 %collective-permute-done.9 = f32[512,128]{1,0:T(8,128)S(1)} collective-permute-done((f32[512,128]{1,0:T(8,128)S(1)}, f32[512,128]{1,0:T(8,128)S(1)}, u32[]{:S(2)}, u32[]{:S(2)}) %collective-permute-start.9) | collective-permute-done | bytes 262176 | tf_op jit(solution)/shard_map/ppermute | solution.py:10
  1026.8 16.1 %collective-permute-start.10 = (f32[256,128]{1,0:T(8,128)S(1)}, f32[256,128]{1,0:T(8,128)S(1)}, u32[]{:S(2)}, u32[]{:S(2)}) collective-permute-start(f32[256,128]{1,0:T(8,128)S(1)} %bitcast.97), channel_id=1, source_target_pairs={{0,16},{4,20},{8,24},{12,28},{16,0},{20,4},{24,8},{28,12},{32,48},... | collective-permute-start | bytes 393224 | tf_op jit(solution)/shard_map/ppermute | solution.py:10
  1042.9 4.4 collective-permute-done.10
  1047.4 1.9 collective-permute-start.11
  1049.3 3.1 collective-permute-done.11
  1052.5 9.6 collective-permute-start.12
  1062.9 11.6 psum.15
  1074.4 6.0 collective-permute-start.13
  1081.4 2.7 collective-permute-start.14
  1084.1 2.3 collective-permute-done.14
  1086.5 1.9 collective-permute-start.15
  1088.5 8.5 collective-permute-done.15
  1097.3 3.8 collective-permute-start.16
  1101.1 24.7 %collective-permute-done.16 = f32[512,128]{1,0:T(8,128)S(1)} collective-permute-done((f32[512,128]{1,0:T(8,128)S(1)}, f32[512,128]{1,0:T(8,128)S(1)}, u32[]{:S(2)}, u32[]{:S(2)}) %collective-permute-start.16) | collective-permute-done | bytes 262176 | tf_op jit(solution)/shard_map/ppermute | solution.py:10
  1126.3 7.0 collective-permute-start.17
  1133.3 45.6 %collective-permute-done.17 = f32[1024,128]{1,0:T(8,128)S(1)} collective-permute-done((f32[1024,128]{1,0:T(8,128)S(1)}, f32[1024,128]{1,0:T(8,128)S(1)}, u32[]{:S(2)}, u32[]{:S(2)}) %collective-permute-start.17) | collective-permute-done | bytes 524320 | tf_op jit(solution)/shard_map/ppermute | solution.py:10
  1179.8 1.9 collective-permute-start.18
  1181.8 24.2 %collective-permute-done.18 = f32[2048,128]{1,0:T(8,128)S(1)} collective-permute-done((f32[2048,128]{1,0:T(8,128)S(1)}, f32[2048,128]{1,0:T(8,128)S(1)}, u32[]{:S(2)}, u32[]{:S(2)}) %collective-permute-start.18) | collective-permute-done | bytes 1048608 | tf_op jit(solution)/shard_map/ppermute | solution.py:10
  1206.3 7.6 copy.72
  (88 shorter events, 19.9 us)
Async XLA Ops:
  8.0 1.0 copy-start
  8.0 716.0 %all-reduce.3.cloned.1.call-start = ((), (), s32[]{:S(2)}) async-start(), calls=%async_computation.1 | async-start | bytes 4194304 | tf_op jit(solution)/shard_map/psum | solution.py:63
  14.4 25.6 %collective-permute-start = (f32[2048,128]{1,0:T(8,128)}, f32[2048,128]{1,0:T(8,128)}, u32[]{:S(2)}, u32[]{:S(2)}) collective-permute-start(f32[2048,128]{1,0:T(8,128)} %constant_dynamic-slice_fusion.12), channel_id=1, source_target_pairs={{0,256},{4,260},{8,264},{12,268},{16,272},{20,276},{24,280},{28,28... | collective-permute-start | bytes 3145736 | tf_op jit(solution)/shard_map/ppermute | solution.py:10
  20.0 20.0 %copy-start.1 = (f32[4096,128]{1,0:T(8,128)S(1)}, f32[4096,128]{1,0:T(8,128)}, u32[]{:S(2)}) copy-start(f32[4096,128]{1,0:T(8,128)} %get-tuple-element.2) | copy-start | bytes 6291460
  41.4 1.5 copy-start.2
  42.9 39.3 %collective-permute-start.1 = (f32[3072,128]{1,0:T(8,128)}, f32[3072,128]{1,0:T(8,128)}, u32[]{:S(2)}, u32[]{:S(2)}) collective-permute-start(f32[3072,128]{1,0:T(8,128)} %pad_maximum_fusion.1), channel_id=1, source_target_pairs={{0,128},{4,132},{8,136},{12,140},{16,144},{20,148},{24,152},{28,15... | collective-permute-start | bytes 4718600 | tf_op jit(solution)/shard_map/ppermute | solution.py:10
  49.0 34.5 %copy-start.3 = (f32[2048,128]{1,0:T(8,128)S(1)}, f32[2048,128]{1,0:T(8,128)}, u32[]{:S(2)}) copy-start(f32[2048,128]{1,0:T(8,128)} %copy-done.2) | copy-start | bytes 3145732
  83.5 1.6 copy-start.4
  85.1 40.0 %collective-permute-start.2 = (f32[1536,128]{1,0:T(8,128)S(1)}, f32[1536,128]{1,0:T(8,128)S(1)}, u32[]{:S(2)}, u32[]{:S(2)}) collective-permute-start(f32[1536,128]{1,0:T(8,128)S(1)} %pad_maximum_fusion.3), channel_id=1, source_target_pairs={{0,64},{4,68},{8,72},{12,76},{16,80},{20,84},{24,88},{28,92},{32,9... | collective-permute-start | bytes 2359304 | tf_op jit(solution)/shard_map/ppermute | solution.py:10
  126.3 113.5 %copy-start.6 = (bf16[4096,8]{0,1:T(8,128)(2,1)S(1)}, bf16[4096,8]{0,1:T(8,128)(2,1)}, u32[]{:S(2)}) copy-start(bf16[4096,8]{0,1:T(8,128)(2,1)} %param.7) | copy-start | bytes 196612
  126.4 77.4 %collective-permute-start.3 = (f32[768,128]{1,0:T(8,128)S(1)}, f32[768,128]{1,0:T(8,128)S(1)}, u32[]{:S(2)}, u32[]{:S(2)}) collective-permute-start(f32[768,128]{1,0:T(8,128)S(1)} %pad_maximum_fusion.5), channel_id=1, source_target_pairs={{0,32},{4,36},{8,40},{12,44},{16,48},{20,52},{24,56},{28,60},{32,0... | collective-permute-start | bytes 1179656 | tf_op jit(solution)/shard_map/ppermute | solution.py:10
  203.9 11.6 collective-permute-start.4
  215.6 5.8 collective-permute-start.5
  221.5 5.2 collective-permute-start.6
  242.2 680.6 %copy-start.7 = (bf16[16,4096]{1,0:T(8,128)(2,1)S(1)}, bf16[16,4096]{1,0:T(8,128)(2,1)}, u32[]{:S(2)}) copy-start(bf16[16,4096]{1,0:T(8,128)(2,1)} %param.9) | copy-start | bytes 393220
  242.2 683.0 %copy-start.5 = (bf16[4096,16]{0,1:T(8,128)(2,1)S(1)}, bf16[4096,16]{0,1:T(8,128)(2,1)}, u32[]{:S(2)}) copy-start(bf16[4096,16]{0,1:T(8,128)(2,1)} %param.8) | copy-start | bytes 393220
  242.2 680.6 %all-gather.2.cloned.1.call-start = ((), (), s32[]{:S(2)}) async-start(), calls=%async_computation.3 | async-start | bytes 2101248 | tf_op jit(solution)/shard_map/all_gather | solution.py:67
  727.2 198.0 %reduce-scatter.2.cloned.1.call-start = ((), (), s32[]{:S(2)}) async-start(), calls=%async_computation.2 | async-start | bytes 40960 | tf_op jit(solution)/shard_map/reduce_scatter | solution.py:60
  932.8 26.5 %collective-permute-start.7 = (f32[2048,128]{1,0:T(8,128)}, f32[2048,128]{1,0:T(8,128)S(1)}, u32[]{:S(2)}, u32[]{:S(2)}) collective-permute-start(f32[2048,128]{1,0:T(8,128)} %bitcast.8), channel_id=1, source_target_pairs={{0,128},{4,132},{8,136},{12,140},{16,144},{20,148},{24,152},{28,15... | collective-permute-start | bytes 3145736 | tf_op jit(solution)/shard_map/ppermute | solution.py:10
  961.4 46.4 %collective-permute-start.8 = (f32[1024,128]{1,0:T(8,128)S(1)}, f32[1024,128]{1,0:T(8,128)S(1)}, u32[]{:S(2)}, u32[]{:S(2)}) collective-permute-start(f32[1024,128]{1,0:T(8,128)S(1)} %bitcast.87), channel_id=1, source_target_pairs={{0,64},{4,68},{8,72},{12,76},{16,80},{20,84},{24,88},{28,92},{32,9... | collective-permute-start | bytes 1572872 | tf_op jit(solution)/shard_map/ppermute | solution.py:10
  1008.3 18.3 %collective-permute-start.9 = (f32[512,128]{1,0:T(8,128)S(1)}, f32[512,128]{1,0:T(8,128)S(1)}, u32[]{:S(2)}, u32[]{:S(2)}) collective-permute-start(f32[512,128]{1,0:T(8,128)S(1)} %bitcast.96), channel_id=1, source_target_pairs={{0,32},{4,36},{8,40},{12,44},{16,48},{20,52},{24,56},{28,60},{32,0... | collective-permute-start | bytes 786440 | tf_op jit(solution)/shard_map/ppermute | solution.py:10
  1026.8 20.5 %collective-permute-start.10 = (f32[256,128]{1,0:T(8,128)S(1)}, f32[256,128]{1,0:T(8,128)S(1)}, u32[]{:S(2)}, u32[]{:S(2)}) collective-permute-start(f32[256,128]{1,0:T(8,128)S(1)} %bitcast.97), channel_id=1, source_target_pairs={{0,16},{4,20},{8,24},{12,28},{16,0},{20,4},{24,8},{28,12},{32,48},... | collective-permute-start | bytes 393224 | tf_op jit(solution)/shard_map/ppermute | solution.py:10
  1047.4 5.0 collective-permute-start.11
  1052.5 10.4 collective-permute-start.12
  1074.4 6.9 collective-permute-start.13
  1081.4 5.0 collective-permute-start.14
  1086.5 10.5 collective-permute-start.15
  1097.3 28.5 %collective-permute-start.16 = (f32[512,128]{1,0:T(8,128)S(1)}, f32[512,128]{1,0:T(8,128)S(1)}, u32[]{:S(2)}, u32[]{:S(2)}) collective-permute-start(f32[512,128]{1,0:T(8,128)S(1)} %bitcast.85), channel_id=1, source_target_pairs={{0,32},{4,36},{8,40},{12,44},{16,48},{20,52},{24,56},{28,60},{32,0... | collective-permute-start | bytes 786440 | tf_op jit(solution)/shard_map/ppermute | solution.py:10
  1126.3 52.6 %collective-permute-start.17 = (f32[1024,128]{1,0:T(8,128)S(1)}, f32[1024,128]{1,0:T(8,128)S(1)}, u32[]{:S(2)}, u32[]{:S(2)}) collective-permute-start(f32[1024,128]{1,0:T(8,128)S(1)} %bitcast.80), channel_id=1, source_target_pairs={{0,64},{4,68},{8,72},{12,76},{16,80},{20,84},{24,88},{28,92},{32,9... | collective-permute-start | bytes 1572872 | tf_op jit(solution)/shard_map/ppermute | solution.py:10
  1179.8 26.1 %collective-permute-start.18 = (f32[2048,128]{1,0:T(8,128)S(1)}, f32[2048,128]{1,0:T(8,128)S(1)}, u32[]{:S(2)}, u32[]{:S(2)}) collective-permute-start(f32[2048,128]{1,0:T(8,128)S(1)} %bitcast.77), channel_id=1, source_target_pairs={{0,128},{4,132},{8,136},{12,140},{16,144},{20,148},{24,152},{28,15... | collective-permute-start | bytes 3145736 | tf_op jit(solution)/shard_map/ppermute | solution.py:10
Sparse Core Ops, SparseCore 0:
  242.3 481.5 all-reduce.2
  729.1 193.6 all-gather.1
Sparse Core Ops, SparseCore 1:
  730.5 23.3 reduce-scatter.1
where the time goes:
time: 1220 us
  waiting for transfers between devices  999 us (82%)
  starting transfers between devices  137 us (11%)
  blocking collectives  24.7 us (2%)
  local copies, waits for them, and re-layouts  17.6 us (1%)
  between operations  16.9 us (1%)
  matrix products  13.9 us (1%)
  other arithmetic  13.5 us (1%)
    psum x1, waiting for transfers between devices, body(): lax.psum(jnp.dot(top_factor, top_block, precision=lax.Precision.HIGHEST),...  482 us
    ppermute x19, waiting for transfers between devices, from_partner(): return lax.ppermute(value, axis, pairs)  323 us
    all_gather x1, waiting for transfers between devices, body(): lax.all_gather(top_adjoint, ('leaf', 'panel'), axis=0, tiled=True)  195 us
    ppermute x19, starting transfers between devices, from_partner(): return lax.ppermute(value, axis, pairs)  136 us
  transfers between devices with their start and end apart: 22, of which 20 were waited for; matrix products, arithmetic and copies ran while one was open for 0% of the time, Pallas kernels for 0%

commit v1 on v0

--- a/solution.py
+++ b/solution.py
@@ -64,7 +64,12 @@
         jnp.dot(top_factor, top_block, precision=lax.Precision.HIGHEST), ("leaf", "panel")
     )
     top_adjoint = jnp.dot(top_factor.T, top_inner, precision=lax.Precision.HIGHEST)
-    top_whole = lax.all_gather(top_adjoint, ("leaf", "panel"), axis=0, tiled=True)
+    top_whole = jnp.concatenate(
+        lax.all_to_all(
+            jnp.stack([top_adjoint] * lax.axis_size(("leaf", "panel"))), ("leaf", "panel"), 0, 0
+        ),
+        axis=0,
+    )
     couple = coupling.astype(jnp.float32)
     mid_rhs = mid_block - jnp.dot(couple, top_whole, precision=lax.Precision.HIGHEST)
     mid_factor = winv_mid.astype(jnp.float32)

time: 1220 us -> 1140 us (0.934)
  waiting for transfers between devices: 999 us -> 927 us
    all_gather x1 -> x0, waiting for transfers between devices: 195 us -> none  [body(): lax.all_gather(top_adjoint, ('leaf', 'panel'), axis=0, tiled=True)]
    all_to_all x0 -> x1, waiting for transfers between devices: none -> 103 us  [body(): lax.all_to_all(jnp.stack([top_adjoint] * lax.axis_size(('leaf', 'panel'))...]
    ppermute x19, starting transfers between devices: 136 us -> 110 us  [from_partner(): return lax.ppermute(value, axis, pairs)]
    ppermute x19, waiting for transfers between devices: 323 us -> 342 us  [from_partner(): return lax.ppermute(value, axis, pairs)]
    all_to_all x0 -> x1, starting transfers between devices: none -> 16.5 us  [body(): lax.all_to_all(jnp.stack([top_adjoint] * lax.axis_size(('leaf', 'panel'))...]
where the time goes in v1:
time: 1140 us
  waiting for transfers between devices  927 us (81%)
  starting transfers between devices  126 us (11%)
  blocking collectives  24.1 us (2%)
  local copies, waits for them, and re-layouts  19.2 us (2%)
  between operations  16.9 us (1%)
  other arithmetic  13.5 us (1%)
  matrix products  11.7 us (1%)
    psum x1, waiting for transfers between devices, body(): lax.psum(jnp.dot(top_factor, top_block, precision=lax.Precision.HIGHEST),...  482 us
    ppermute x19, waiting for transfers between devices, from_partner(): return lax.ppermute(value, axis, pairs)  342 us
    ppermute x19, starting transfers between devices, from_partner(): return lax.ppermute(value, axis, pairs)  110 us
    all_to_all x1, waiting for transfers between devices, body(): lax.all_to_all(jnp.stack([top_adjoint] * lax.axis_size(('leaf', 'panel'))...  103 us
  transfers between devices with their start and end apart: 22, of which 20 were waited for; matrix products, arithmetic and copies ran while one was open for 0% of the time, Pallas kernels for 0%

profile of v1, /device:TPU:1, one launch (start us, length us, event | category | flops | bytes accessed | tf_op | source)
XLA Modules:
  0.0 1138.2 jit_solution(10445743963526704984)
XLA Ops:
  10.5 1.6 fusion.11
  12.1 2.3 constant_dynamic-slice_fusion.12
  14.4 5.6 collective-permute-start
  20.1 19.9 %collective-permute-done = f32[2048,128]{1,0:T(8,128)} collective-permute-done((f32[2048,128]{1,0:T(8,128)}, f32[2048,128]{1,0:T(8,128)}, u32[]{:S(2)}, u32[]{:S(2)}) %collective-permute-start) | collective-permute-done | bytes 1048608 | tf_op jit(solution)/shard_map/ppermute | solution.py:10
  42.8 6.2 collective-permute-start.1
  49.0 33.1 %collective-permute-done.1 = f32[3072,128]{1,0:T(8,128)} collective-permute-done((f32[3072,128]{1,0:T(8,128)}, f32[3072,128]{1,0:T(8,128)}, u32[]{:S(2)}, u32[]{:S(2)}) %collective-permute-start.1) | collective-permute-done | bytes 1572896 | tf_op jit(solution)/shard_map/ppermute | solution.py:10
  85.1 15.7 %collective-permute-start.2 = (f32[1536,128]{1,0:T(8,128)S(1)}, f32[1536,128]{1,0:T(8,128)S(1)}, u32[]{:S(2)}, u32[]{:S(2)}) collective-permute-start(f32[1536,128]{1,0:T(8,128)S(1)} %pad_maximum_fusion.3), channel_id=1, source_target_pairs={{0,64},{4,68},{8,72},{12,76},{16,80},{20,84},{24,88},{28,92},{32,9... | collective-permute-start | bytes 2359304 | tf_op jit(solution)/shard_map/ppermute | solution.py:10
  100.8 24.3 %collective-permute-done.2 = f32[1536,128]{1,0:T(8,128)S(1)} collective-permute-done((f32[1536,128]{1,0:T(8,128)S(1)}, f32[1536,128]{1,0:T(8,128)S(1)}, u32[]{:S(2)}, u32[]{:S(2)}) %collective-permute-start.2) | collective-permute-done | bytes 786464 | tf_op jit(solution)/shard_map/ppermute | solution.py:10
  126.3 38.8 %collective-permute-start.3 = (f32[768,128]{1,0:T(8,128)S(1)}, f32[768,128]{1,0:T(8,128)S(1)}, u32[]{:S(2)}, u32[]{:S(2)}) collective-permute-start(f32[768,128]{1,0:T(8,128)S(1)} %pad_maximum_fusion.5), channel_id=1, source_target_pairs={{0,32},{4,36},{8,40},{12,44},{16,48},{20,52},{24,56},{28,60},{32,0... | collective-permute-start | bytes 1179656 | tf_op jit(solution)/shard_map/ppermute | solution.py:10
  165.2 38.6 %collective-permute-done.3 = f32[768,128]{1,0:T(8,128)S(1)} collective-permute-done((f32[768,128]{1,0:T(8,128)S(1)}, f32[768,128]{1,0:T(8,128)S(1)}, u32[]{:S(2)}, u32[]{:S(2)}) %collective-permute-start.3) | collective-permute-done | bytes 393248 | tf_op jit(solution)/shard_map/ppermute | solution.py:10
  203.9 1.9 collective-permute-start.4
  205.8 9.6 collective-permute-done.4
  215.6 1.9 collective-permute-start.5
  217.5 3.8 collective-permute-done.5
  221.4 3.3 collective-permute-start.6
  226.6 13.1 %all-reduce = f32[32,128]{1,0:T(8,128)S(1)} all-reduce(f32[32,128]{1,0:T(8,128)S(1)} %slice_add_fusion.11), channel_id=2, replica_groups=mesh['leaf'=128,'panel'=4] {'panel'}, use_global_device_ids=true, to_apply=%region_0.0.clone | all-reduce | flops 4096 | bytes 32768
  239.8 2.4 convolution_bitcast_fusion.1
  242.2 481.8 %all-reduce.3.cloned.1.call-done = f32[4096,128]{0,1:T(8,128)} async-done(((f32[4096,128]{0,1:T(8,128)}), f32[4096,128]{0,1:T(8,128)}) %all-reduce.3.cloned.1.call-update) | async-done | bytes 2097168 | tf_op jit(solution)/shard_map/psum | solution.py:63
  723.9 2.6 convolution_bitcast_fusion.3
  728.1 16.5 %all-to-all-start = ((f32[512,8,128]{2,1,0:T(8,128)}), f32[512,8,128]{2,1,0:T(8,128)S(1)}, u32[]{:S(2)}, u32[]{:S(2)}) async-start(f32[512,8,128]{2,1,0:T(8,128)} %stack.38), calls=%async_computation.1 | async-start | bytes 4194304 | tf_op jit(solution)/shard_map/all_to_all | solution.py:68
  745.3 102.6 %all-to-all-done = f32[512,8,128]{2,1,0:T(8,128)S(1)} async-done(((f32[512,8,128]{2,1,0:T(8,128)}), f32[512,8,128]{2,1,0:T(8,128)S(1)}, u32[]{:S(2)}, u32[]{:S(2)}) %all-to-all-start) | async-done | bytes 2097184 | tf_op jit(solution)/shard_map/all_to_all | solution.py:68
  848.7 3.1 convolution_bitcast_fusion
  851.8 1.9 copy.66
  853.7 2.5 broadcast_select_fusion
  856.3 1.9 collective-permute-start.7
  858.2 24.6 %collective-permute-done.7 = f32[2048,128]{1,0:T(8,128)S(1)} collective-permute-done((f32[2048,128]{1,0:T(8,128)}, f32[2048,128]{1,0:T(8,128)S(1)}, u32[]{:S(2)}, u32[]{:S(2)}) %collective-permute-start.7) | collective-permute-done | bytes 1048608 | tf_op jit(solution)/shard_map/ppermute | solution.py:10
  884.9 3.3 collective-permute-start.8
  888.2 53.6 %collective-permute-done.8 = f32[1024,128]{1,0:T(8,128)S(1)} collective-permute-done((f32[1024,128]{1,0:T(8,128)S(1)}, f32[1024,128]{1,0:T(8,128)S(1)}, u32[]{:S(2)}, u32[]{:S(2)}) %collective-permute-start.8) | collective-permute-done | bytes 524320 | tf_op jit(solution)/shard_map/ppermute | solution.py:10
  942.2 1.9 collective-permute-start.9
  944.2 20.9 %collective-permute-done.9 = f32[512,128]{1,0:T(8,128)S(1)} collective-permute-done((f32[512,128]{1,0:T(8,128)S(1)}, f32[512,128]{1,0:T(8,128)S(1)}, u32[]{:S(2)}, u32[]{:S(2)}) %collective-permute-start.9) | collective-permute-done | bytes 262176 | tf_op jit(solution)/shard_map/ppermute | solution.py:10
  965.3 1.9 collective-permute-start.10
  967.3 5.4 collective-permute-done.10
  972.8 1.9 collective-permute-start.11
  974.8 3.1 collective-permute-done.11
  977.9 4.4 collective-permute-start.12
  983.2 10.9 psum.15
  994.1 5.7 collective-permute-start.13
  1000.8 1.9 collective-permute-start.14
  1002.7 3.1 collective-permute-done.14
  1005.9 1.9 collective-permute-start.15
  1007.9 8.9 collective-permute-done.15
  1017.0 2.5 collective-permute-start.16
  1019.6 24.8 %collective-permute-done.16 = f32[512,128]{1,0:T(8,128)S(1)} collective-permute-done((f32[512,128]{1,0:T(8,128)S(1)}, f32[512,128]{1,0:T(8,128)S(1)}, u32[]{:S(2)}, u32[]{:S(2)}) %collective-permute-start.16) | collective-permute-done | bytes 262176 | tf_op jit(solution)/shard_map/ppermute | solution.py:10
  1044.8 7.0 collective-permute-start.17
  1051.8 42.5 %collective-permute-done.17 = f32[1024,128]{1,0:T(8,128)S(1)} collective-permute-done((f32[1024,128]{1,0:T(8,128)S(1)}, f32[1024,128]{1,0:T(8,128)S(1)}, u32[]{:S(2)}, u32[]{:S(2)}) %collective-permute-start.17) | collective-permute-done | bytes 524320 | tf_op jit(solution)/shard_map/ppermute | solution.py:10
  1095.3 1.9 collective-permute-start.18
  1097.2 24.2 %collective-permute-done.18 = f32[2048,128]{1,0:T(8,128)S(1)} collective-permute-done((f32[2048,128]{1,0:T(8,128)S(1)}, f32[2048,128]{1,0:T(8,128)S(1)}, u32[]{:S(2)}, u32[]{:S(2)}) %collective-permute-start.18) | collective-permute-done | bytes 1048608 | tf_op jit(solution)/shard_map/ppermute | solution.py:10
  1121.7 7.6 copy.72
  (90 shorter events, 22.2 us)
Async XLA Ops:
  8.0 1.0 copy-start
  8.0 715.9 %all-reduce.3.cloned.1.call-start = ((), (), s32[]{:S(2)}) async-start(), calls=%async_computation.2 | async-start | bytes 4194304 | tf_op jit(solution)/shard_map/psum | solution.py:63
  14.4 25.6 %collective-permute-start = (f32[2048,128]{1,0:T(8,128)}, f32[2048,128]{1,0:T(8,128)}, u32[]{:S(2)}, u32[]{:S(2)}) collective-permute-start(f32[2048,128]{1,0:T(8,128)} %constant_dynamic-slice_fusion.12), channel_id=1, source_target_pairs={{0,256},{4,260},{8,264},{12,268},{16,272},{20,276},{24,280},{28,28... | collective-permute-start | bytes 3145736 | tf_op jit(solution)/shard_map/ppermute | solution.py:10
  20.0 20.0 %copy-start.1 = (f32[4096,128]{1,0:T(8,128)S(1)}, f32[4096,128]{1,0:T(8,128)}, u32[]{:S(2)}) copy-start(f32[4096,128]{1,0:T(8,128)} %get-tuple-element.2) | copy-start | bytes 6291460
  41.3 1.5 copy-start.2
  42.8 39.3 %collective-permute-start.1 = (f32[3072,128]{1,0:T(8,128)}, f32[3072,128]{1,0:T(8,128)}, u32[]{:S(2)}, u32[]{:S(2)}) collective-permute-start(f32[3072,128]{1,0:T(8,128)} %pad_maximum_fusion.1), channel_id=1, source_target_pairs={{0,128},{4,132},{8,136},{12,140},{16,144},{20,148},{24,152},{28,15... | collective-permute-start | bytes 4718600 | tf_op jit(solution)/shard_map/ppermute | solution.py:10
  49.0 34.5 %copy-start.3 = (f32[2048,128]{1,0:T(8,128)S(1)}, f32[2048,128]{1,0:T(8,128)}, u32[]{:S(2)}) copy-start(f32[2048,128]{1,0:T(8,128)} %copy-done.2) | copy-start | bytes 3145732
  83.5 1.6 copy-start.4
  85.1 40.0 %collective-permute-start.2 = (f32[1536,128]{1,0:T(8,128)S(1)}, f32[1536,128]{1,0:T(8,128)S(1)}, u32[]{:S(2)}, u32[]{:S(2)}) collective-permute-start(f32[1536,128]{1,0:T(8,128)S(1)} %pad_maximum_fusion.3), channel_id=1, source_target_pairs={{0,64},{4,68},{8,72},{12,76},{16,80},{20,84},{24,88},{28,92},{32,9... | collective-permute-start | bytes 2359304 | tf_op jit(solution)/shard_map/ppermute | solution.py:10
  126.3 113.5 %copy-start.6 = (bf16[4096,8]{0,1:T(8,128)(2,1)S(1)}, bf16[4096,8]{0,1:T(8,128)(2,1)}, u32[]{:S(2)}) copy-start(bf16[4096,8]{0,1:T(8,128)(2,1)} %param.7) | copy-start | bytes 196612
  126.3 77.4 %collective-permute-start.3 = (f32[768,128]{1,0:T(8,128)S(1)}, f32[768,128]{1,0:T(8,128)S(1)}, u32[]{:S(2)}, u32[]{:S(2)}) collective-permute-start(f32[768,128]{1,0:T(8,128)S(1)} %pad_maximum_fusion.5), channel_id=1, source_target_pairs={{0,32},{4,36},{8,40},{12,44},{16,48},{20,52},{24,56},{28,60},{32,0... | collective-permute-start | bytes 1179656 | tf_op jit(solution)/shard_map/ppermute | solution.py:10
  203.9 11.6 %collective-permute-start.4 = (f32[384,128]{1,0:T(8,128)S(1)}, f32[384,128]{1,0:T(8,128)S(1)}, u32[]{:S(2)}, u32[]{:S(2)}) collective-permute-start(f32[384,128]{1,0:T(8,128)S(1)} %pad_maximum_fusion.7), channel_id=1, source_target_pairs={{0,16},{4,20},{8,24},{12,28},{16,0},{20,4},{24,8},{28,12},{32,48},... | collective-permute-start | bytes 589832 | tf_op jit(solution)/shard_map/ppermute | solution.py:10
  215.6 5.8 collective-permute-start.5
  221.4 5.2 collective-permute-start.6
  726.5 1.5 copy-start.8
  728.1 119.8 %copy-start.7 = (bf16[16,4096]{1,0:T(8,128)(2,1)S(1)}, bf16[16,4096]{1,0:T(8,128)(2,1)}, u32[]{:S(2)}) copy-start(bf16[16,4096]{1,0:T(8,128)(2,1)} %param.9) | copy-start | bytes 393220
  728.1 119.8 %all-to-all-start = ((f32[512,8,128]{2,1,0:T(8,128)}), f32[512,8,128]{2,1,0:T(8,128)S(1)}, u32[]{:S(2)}, u32[]{:S(2)}) async-start(f32[512,8,128]{2,1,0:T(8,128)} %stack.38), calls=%async_computation.1 | async-start | bytes 4194304 | tf_op jit(solution)/shard_map/all_to_all | solution.py:68
  744.6 104.2 %copy-start.5 = (bf16[4096,16]{0,1:T(8,128)(2,1)S(1)}, bf16[4096,16]{0,1:T(8,128)(2,1)}, u32[]{:S(2)}) copy-start(bf16[4096,16]{0,1:T(8,128)(2,1)} %param.8) | copy-start | bytes 393220
  744.6 104.1 %reduce-scatter.2.cloned.1.call-start = ((), (), s32[]{:S(2)}) async-start(), calls=%async_computation.3 | async-start | bytes 40960 | tf_op jit(solution)/shard_map/reduce_scatter | solution.py:60
  856.3 26.6 %collective-permute-start.7 = (f32[2048,128]{1,0:T(8,128)}, f32[2048,128]{1,0:T(8,128)S(1)}, u32[]{:S(2)}, u32[]{:S(2)}) collective-permute-start(f32[2048,128]{1,0:T(8,128)} %bitcast.9), channel_id=1, source_target_pairs={{0,128},{4,132},{8,136},{12,140},{16,144},{20,148},{24,152},{28,15... | collective-permute-start | bytes 3145736 | tf_op jit(solution)/shard_map/ppermute | solution.py:10
  884.9 56.9 %collective-permute-start.8 = (f32[1024,128]{1,0:T(8,128)S(1)}, f32[1024,128]{1,0:T(8,128)S(1)}, u32[]{:S(2)}, u32[]{:S(2)}) collective-permute-start(f32[1024,128]{1,0:T(8,128)S(1)} %bitcast.91), channel_id=1, source_target_pairs={{0,64},{4,68},{8,72},{12,76},{16,80},{20,84},{24,88},{28,92},{32,9... | collective-permute-start | bytes 1572872 | tf_op jit(solution)/shard_map/ppermute | solution.py:10
  942.2 22.9 %collective-permute-start.9 = (f32[512,128]{1,0:T(8,128)S(1)}, f32[512,128]{1,0:T(8,128)S(1)}, u32[]{:S(2)}, u32[]{:S(2)}) collective-permute-start(f32[512,128]{1,0:T(8,128)S(1)} %bitcast.100), channel_id=1, source_target_pairs={{0,32},{4,36},{8,40},{12,44},{16,48},{20,52},{24,56},{28,60},{32,0... | collective-permute-start | bytes 786440 | tf_op jit(solution)/shard_map/ppermute | solution.py:10
  965.3 7.4 collective-permute-start.10
  972.8 5.0 collective-permute-start.11
  977.9 5.3 collective-permute-start.12
  994.1 6.6 collective-permute-start.13
  1000.8 5.0 collective-permute-start.14
  1005.9 10.8 collective-permute-start.15
  1017.0 27.3 %collective-permute-start.16 = (f32[512,128]{1,0:T(8,128)S(1)}, f32[512,128]{1,0:T(8,128)S(1)}, u32[]{:S(2)}, u32[]{:S(2)}) collective-permute-start(f32[512,128]{1,0:T(8,128)S(1)} %bitcast.89), channel_id=1, source_target_pairs={{0,32},{4,36},{8,40},{12,44},{16,48},{20,52},{24,56},{28,60},{32,0... | collective-permute-start | bytes 786440 | tf_op jit(solution)/shard_map/ppermute | solution.py:10
  1044.8 49.5 %collective-permute-start.17 = (f32[1024,128]{1,0:T(8,128)S(1)}, f32[1024,128]{1,0:T(8,128)S(1)}, u32[]{:S(2)}, u32[]{:S(2)}) collective-permute-start(f32[1024,128]{1,0:T(8,128)S(1)} %bitcast.84), channel_id=1, source_target_pairs={{0,64},{4,68},{8,72},{12,76},{16,80},{20,84},{24,88},{28,92},{32,9... | collective-permute-start | bytes 1572872 | tf_op jit(solution)/shard_map/ppermute | solution.py:10
  1095.3 26.1 %collective-permute-start.18 = (f32[2048,128]{1,0:T(8,128)S(1)}, f32[2048,128]{1,0:T(8,128)S(1)}, u32[]{:S(2)}, u32[]{:S(2)}) collective-permute-start(f32[2048,128]{1,0:T(8,128)S(1)} %bitcast.81), channel_id=1, source_target_pairs={{0,128},{4,132},{8,136},{12,140},{16,144},{20,148},{24,152},{28,15... | collective-permute-start | bytes 3145736 | tf_op jit(solution)/shard_map/ppermute | solution.py:10
Sparse Core Ops, SparseCore 0:
  242.3 481.5 all-reduce.2
Sparse Core Ops, SparseCore 1:
  747.8 29.0 reduce-scatter.1
